TPU v7x, 32 devices: a whole 2x2x4 slice. The times are simulated.
32 devices in a mesh: gx: 4 (over y, x), gy: 8 (over z, core).
Axes of the slice: x: 2, y: 2, z: 4, core: 2. Of those that a mesh axis runs over, the one named last changes fastest.
Arguments:
- basis_fields: float32 [128, 128, 1024], P(None, 'gx', 'gy'), may hold values from -6 to 6
- carried_fields: float32 [128, 128, 1024], P(None, 'gx', 'gy'), may hold values from -70 to 70, as said below
- velocity: float32 [2, 128, 1024], P(None, 'gx', 'gy'), may hold values from -1 to 1
- diffusion: float32 [128, 128], replicated, may hold values from -0.024 to 0.09, as said below
- advection: float32 [128, 128], replicated, may hold values from -0.18 to 0.18
Outputs:
- new_basis: float32 [256, 128, 1024], P(None, 'gx', 'gy')
- galerkin: float32 [256, 128], replicated
Inputs may be any that keep to these rules, and one draw needn't show every extreme that they name: `carried_fields`: entries of the field block are of order one with scales varying over cells and fields. `diffusion`: A positive diagonal with small couplings off it.
All inputs are finite; a program needn't handle non-finite values.
Results may differ from a plain program's by a relative error of at most 0.000086.
Values sent between devices are 32-bit elements; how exact they have to be, the bound alone decides.
No kernel may reach another device: no remote copies, remote signals or barrier semaphores. Data moves between devices by JAX's collectives and lax.ppermute only.
A program may use at most 64 MiB of HBM per device.

v0:
```python
import jax
import jax.numpy as jnp
from jax import lax
from jax.sharding import PartitionSpec as P


def extended(array, sides, width):
    for axis, dim in sides:
        count, length = (lax.axis_size(axis), array.shape[dim])
        up = [(i, (i + 1) % count) for i in range(count)]
        down = [(j, i) for i, j in up]
        last = lax.slice_in_dim(array, length - width, length, axis=dim)
        first = lax.slice_in_dim(array, 0, width, axis=dim)
        before = lax.ppermute(last, axis, up)
        after = lax.ppermute(first, axis, down)
        array = jnp.concatenate([before, array, after], axis=dim)
    return array


def field_rate(padded, velocity, diffusion, advection):
    center = padded[:, 1:-1, 1:-1]
    plus_x = padded[:, 2:, 1:-1]
    minus_x = padded[:, :-2, 1:-1]
    plus_y = padded[:, 1:-1, 2:]
    minus_y = padded[:, 1:-1, :-2]
    field_shape = center.shape
    laplace = plus_x + minus_x + plus_y + minus_y - 4.0 * center
    transport = velocity[0] * (plus_x - minus_x) * 0.5 + velocity[1] * (plus_y - minus_y) * 0.5
    spread_part = jnp.dot(
        diffusion.T, laplace.reshape(field_shape[0], -1), precision=lax.Precision.HIGHEST
    )
    carry_part = jnp.dot(
        advection.T, transport.reshape(field_shape[0], -1), precision=lax.Precision.HIGHEST
    )
    return (spread_part - carry_part).reshape(field_shape)


def one_substep(fields, velocity, diffusion, advection):
    padded = extended(fields, (("gx", 1), ("gy", 2)), 1)
    return fields + field_rate(padded, velocity, diffusion, advection)


def body(basis_fields, carried_fields, velocity, diffusion, advection):
    basis_rank, tile_rows, tile_cols = carried_fields.shape
    tile_cells = tile_rows * tile_cols
    aug_count = 2 * basis_rank
    cell_weight = 1.0 / (tile_cells * lax.axis_size("gx") * lax.axis_size("gy"))
    flat_basis = basis_fields.reshape(basis_rank, tile_cells)
    flat_carried = carried_fields.reshape(basis_rank, tile_cells)
    section_one = one_substep(carried_fields, velocity, diffusion, advection)
    section_two = one_substep(section_one, velocity, diffusion, advection)
    flat_new = section_two.reshape(basis_rank, tile_cells)
    stacked = jnp.concatenate([flat_basis, flat_new], 0)
    whole_sum = lax.psum(jnp.dot(stacked, stacked.T, precision=lax.Precision.HIGHEST), ("gx", "gy"))
    gram_matrix = whole_sum * cell_weight
    cholesky_low = jnp.linalg.cholesky(gram_matrix)
    identity = jnp.eye(aug_count, dtype=jnp.float32)
    inverse = jax.scipy.linalg.solve_triangular(cholesky_low, identity, lower=True)
    new_basis = jnp.dot(inverse, stacked, precision=lax.Precision.HIGHEST)
    galerkin = (
        lax.psum(jnp.dot(new_basis, flat_carried.T, precision=lax.Precision.HIGHEST), ("gx", "gy"))
        * cell_weight
    )
    return (new_basis.reshape(aug_count, tile_rows, tile_cols), galerkin)


def solution(mesh):
    in_specs = (P(None, "gx", "gy"), P(None, "gx", "gy"), P(None, "gx", "gy"), P(), P())
    out_specs = (P(None, "gx", "gy"), P())
    return jax.shard_map(body, mesh=mesh, in_specs=in_specs, out_specs=out_specs, check_vma=False)
```

profile of v0, /device:TPU:0, one launch (start us, length us, event | category | flops | bytes accessed | tf_op | source)
XLA Modules:
  0.0 395.5 jit_solution(6625425687016328248)
XLA Ops:
  7.2 2.0 copy.49
  9.3 3.0 collective-permute-start.1
  13.3 3.5 copy.42
  17.0 1.9 pad_maximum_fusion.3
  18.9 2.7 collective-permute-start.2
  23.2 3.5 collective-permute-done.3
  26.7 2.7 add_multiply_fusion.1
  29.4 1.9 fusion.22
  31.3 1.9 convolution_subtract_fusion.1
  33.5 1.6 collective-permute-start.4
  35.6 2.2 collective-permute-done.4
  37.8 2.5 collective-permute-done.5
  41.2 3.0 copy.36
  44.2 1.6 collective-permute-done.7
  45.8 2.8 multiply_subtract_fusion
  48.6 1.8 fusion.23
  50.5 4.2 %add_multiply_fusion = f32[128,32,128]{0,2,1:T(8,128)S(1)} fusion(f32[128,1,128]{0,2,1:T(8,128)S(1)} %collective-permute-done.4, f32[128,32,128]{0,2,1:T(8,128)S(1)} %add.63, f32[128,1,128]{0,2,1:T(8,128)S(1)} %collective-permute-done.5, f32[128,34,1]{0,2,1:T(1,128)S(1)} %copy.51, f32[128,34,1]{0,2,1:T(1,128)S(1)} %copy.53, ...), kind=kLoop, calls=%fused_computation.23 | loop fusion | flops 7340032 | bytes 4392960 | tf_op jit(solution)/shard_map/add | solution.py:28
  54.7 1.9 convolution_subtract_fusion
  58.9 7.4 %fusion.1 = f32[256,256]{0,1:T(8,128)} fusion(f32[128,4096]{0,1:T(8,128)S(1)} %bitcast.71, f32[128,4096]{0,1:T(8,128)S(1)} %bitcast.75), kind=kOutput, calls=%fused_computation.6 | convolution fusion | flops 3222274048 | bytes 4456448 | tf_op jit(solution)/shard_map/dot_general | solution.py:54
  66.6 123.1 %all-reduce.4.cloned.1.call-done = f32[256,256]{0,1:T(8,128)} async-done(((f32[256,256]{0,1:T(8,128)}), f32[256,256]{0,1:T(8,128)}) %all-reduce.4.cloned.1.call-update) | async-done | bytes 262160 | tf_op jit(solution)/shard_map/psum | solution.py:54
  192.0 11.7 %cholesky.50 = f32[128,128]{1,0:T(8,128)S(1)} custom-call(f32[128,128]{1,0:T(8,128)S(1)} %cholesky.118), custom_call_target="Cholesky" | custom-call | tf_op jit(solution)/shard_map/jit(cholesky)/cholesky | solution.py:56
  203.8 9.8 %custom-call.15 = f32[1,128,128]{1,2,0:T(8,128)S(1)} custom-call(f32[1,128,128]{2,1,0:T(8,128)S(1)} %get-tuple-element.33), custom_call_target="InvertDiagBlocksLowerTriangular" | custom-call | tf_op jit(solution)/shard_map/jit(cholesky)/cholesky | solution.py:56
  214.1 11.7 %cholesky.105 = f32[128,128]{1,0:T(8,128)S(1)} custom-call(f32[128,128]{1,0:T(8,128)S(1)} %convolution_subtract_fusion.3), custom_call_target="Cholesky" | custom-call | tf_op jit(solution)/shard_map/jit(cholesky)/cholesky | solution.py:56
  227.9 4.1 %while.1 = (s32[]{:T(128)}, f32[256,256]{1,0:T(8,128)S(1)}, s32[2,2]{1,0:T(2,128)S(1)}, f32[2,128,128]{2,1,0:T(8,128)S(1)}, s32[]{:T(128)}) while((s32[]{:T(128)}, f32[256,256]{1,0:T(8,128)S(1)}, s32[2,2]{1,0:T(2,128)S(1)}, f32[2,128,128]{2,1,0:T(8,128)S(1)}, s32[]{:T(128)}) %tuple.33), condition=%wide.while_cond, body=%wide.while_body.sunk | while | flops 2 | bytes 131181 | solution.py:58
  228.7 1.3 bitcast_dynamic-update-slice_fusion.2
  232.0 19.7 %custom-call.16 = f32[2,128,128]{1,2,0:T(8,128)S(1)} custom-call(f32[2,128,128]{2,1,0:T(8,128)S(1)} %get-tuple-element.9), custom_call_target="InvertDiagBlocksLowerTriangular" | custom-call | tf_op jit(solution)/shard_map/jit(_solve_triangular)/triangular_solve | solution.py:58
  252.6 5.8 %fusion = f32[256,4096]{1,0:T(8,128)S(1)} fusion(f32[128,4096]{0,1:T(8,128)S(1)} %bitcast.72, f32[128,4096]{0,1:T(8,128)} %bitcast.74, f32[128,256]{1,0:T(8,128)S(1)} %fusion.12, f32[128,256]{1,0:T(8,128)S(1)} %fusion.9), kind=kOutput, calls=%fused_computation.5 | convolution fusion | flops 3222339584 | bytes 8650752 | tf_op jit(solution)/shard_map/dot_general | solution.py:59
  258.4 1.9 copy-done.1
  260.3 4.9 %fusion.2 = f32[256,128]{1,0:T(8,128)} fusion(f32[256,4096]{1,0:T(8,128)S(1)} %fusion, f32[16,8,32,128]{3,2,1,0:T(8,128)S(1)} %bitcast.65), kind=kOutput, calls=%fused_computation.8 | convolution fusion | flops 1610612736 | bytes 6422528 | tf_op jit(solution)/shard_map/dot_general | solution.py:61
  265.3 5.0 %copy.57 = f32[32,8,32,128]{3,2,1,0:T(8,128)} copy(f32[32,8,32,128]{3,1,2,0:T(8,128)} %bitcast.64) | data formatting | bytes 8388608
  270.2 116.6 %all-reduce.6.cloned.1.call-done = f32[256,128]{1,0:T(8,128)} async-done(((f32[256,128]{1,0:T(8,128)}), f32[256,128]{1,0:T(8,128)}) %all-reduce.6.cloned.1.call-update) | async-done | bytes 131088 | tf_op jit(solution)/shard_map/psum | solution.py:61
  386.9 1.6 broadcast_multiply_fusion.1
  (69 shorter events, 14.1 us)
Async XLA Ops:
  7.2 22.2 %copy-start = (f32[128,128]{1,0:T(8,128)S(1)}, f32[128,128]{1,0:T(8,128)}, u32[]{:S(2)}) copy-start(f32[128,128]{1,0:T(8,128)} %param.8) | copy-start | bytes 196612
  7.2 182.6 %all-reduce.4.cloned.1.call-start = ((), (), s32[]{:S(2)}) async-start(), calls=%async_computation | async-start | bytes 524288 | tf_op jit(solution)/shard_map/psum | solution.py:54
  9.2 17.4 %copy-start.2 = (f32[128,32,128]{0,2,1:T(8,128)}, f32[128,32,128]{0,2,1:T(8,128)S(1)}, u32[]{:S(2)}) copy-start(f32[128,32,128]{0,2,1:T(8,128)S(1)} %copy.49) | copy-start | bytes 6291460
  9.3 7.5 %collective-permute-start.1 = (f32[128,1,128]{0,2,1:T(8,128)S(1)}, f32[128,1,128]{0,2,1:T(8,128)S(1)}, u32[]{:S(2)}, u32[]{:S(2)}) collective-permute-start(f32[128,1,128]{0,2,1:T(8,128)S(1)} %get-tuple-element.28), channel_id=1, source_target_pairs={{0,8},{8,16},{16,24},{24,0},{1,9},{9,17},{17,25},{25,1},{2,10},{10... | collective-permute-start | bytes 196616 | tf_op jit(solution)/shard_map/ppermute | solution.py:14
  12.3 4.7 %collective-permute-start = (f32[128,1,128]{0,2,1:T(8,128)S(1)}, f32[128,1,128]{0,2,1:T(8,128)S(1)}, u32[]{:S(2)}, u32[]{:S(2)}) collective-permute-start(f32[128,1,128]{0,2,1:T(8,128)S(1)} %get-tuple-element.29), channel_id=1, source_target_pairs={{8,0},{16,8},{24,16},{0,24},{9,1},{17,9},{25,17},{1,25},{10,2},{18... | collective-permute-start | bytes 196616 | tf_op jit(solution)/shard_map/ppermute | solution.py:15
  17.0 4.7 %copy-start.9 = (f32[2,32,128]{2,1,0:T(8,128)S(1)}, f32[2,32,128]{2,1,0:T(8,128)}, u32[]{:S(2)}) copy-start(f32[2,32,128]{2,1,0:T(8,128)} %param.7) | copy-start | bytes 98308
  18.9 4.2 %collective-permute-start.2 = (f32[128,34,1]{0,1,2:T(8,128)S(1)}, f32[128,34,1]{0,1,2:T(8,128)S(1)}, u32[]{:S(2)}, u32[]{:S(2)}) collective-permute-start(f32[128,34,1]{0,1,2:T(8,128)S(1)} %get-tuple-element.23), channel_id=1, source_target_pairs={{1,0},{2,1},{3,2},{4,3},{5,4},{6,5},{7,6},{0,7},{9,8},{10,9},{11,1... | collective-permute-start | bytes 52232 | tf_op jit(solution)/shard_map/ppermute | solution.py:15
  21.7 5.0 %collective-permute-start.3 = (f32[128,34,1]{0,1,2:T(8,128)S(1)}, f32[128,34,1]{0,1,2:T(8,128)S(1)}, u32[]{:S(2)}, u32[]{:S(2)}) collective-permute-start(f32[128,34,1]{0,1,2:T(8,128)S(1)} %get-tuple-element.22), channel_id=1, source_target_pairs={{0,1},{1,2},{2,3},{3,4},{4,5},{5,6},{6,7},{7,0},{8,9},{9,10},{10,1... | collective-permute-start | bytes 52232 | tf_op jit(solution)/shard_map/ppermute | solution.py:14
  29.4 1.9 copy-start.8
  31.3 1.9 copy-start.3
  33.5 4.3 %collective-permute-start.4 = (f32[128,1,128]{0,2,1:T(8,128)S(1)}, f32[128,1,128]{0,2,1:T(8,128)S(1)}, u32[]{:S(2)}, u32[]{:S(2)}) collective-permute-start(f32[128,1,128]{0,2,1:T(8,128)S(1)} %get-tuple-element.27), channel_id=1, source_target_pairs={{8,0},{16,8},{24,16},{0,24},{9,1},{17,9},{25,17},{1,25},{10,2},{18... | collective-permute-start | bytes 196616 | tf_op jit(solution)/shard_map/ppermute | solution.py:15
  35.1 5.2 %collective-permute-start.5 = (f32[128,1,128]{0,2,1:T(8,128)S(1)}, f32[128,1,128]{0,2,1:T(8,128)S(1)}, u32[]{:S(2)}, u32[]{:S(2)}) collective-permute-start(f32[128,1,128]{0,2,1:T(8,128)S(1)} %get-tuple-element.26), channel_id=1, source_target_pairs={{0,8},{8,16},{16,24},{24,0},{1,9},{9,17},{17,25},{25,1},{2,10},{10... | collective-permute-start | bytes 196616 | tf_op jit(solution)/shard_map/ppermute | solution.py:14
  40.3 3.8 collective-permute-start.6
  40.4 5.3 %collective-permute-start.7 = (f32[128,34,1]{0,1,2:T(8,128)S(1)}, f32[128,34,1]{0,1,2:T(8,128)S(1)}, u32[]{:S(2)}, u32[]{:S(2)}) collective-permute-start(f32[128,34,1]{0,1,2:T(8,128)S(1)} %copy.52), channel_id=1, source_target_pairs={{0,1},{1,2},{2,3},{3,4},{4,5},{5,6},{6,7},{7,0},{8,9},{9,10},{10,1... | collective-permute-start | bytes 52232 | tf_op jit(solution)/shard_map/ppermute | solution.py:14
  56.5 2.3 copy-start.7
  56.9 1.3 copy-start.5
  66.3 320.5 %all-reduce.6.cloned.1.call-start = ((), (), s32[]{:S(2)}) async-start(), calls=%async_computation.1 | async-start | bytes 262144 | tf_op jit(solution)/shard_map/psum | solution.py:61
  190.9 61.7 %copy-start.6 = (f32[128,32,128]{0,2,1:T(8,128)S(1)}, f32[128,32,128]{0,2,1:T(8,128)}, u32[]{:S(2)}) copy-start(f32[128,32,128]{0,2,1:T(8,128)} %copy-done.5) | copy-start | bytes 6291460
  252.6 7.8 %copy-start.4 = (f32[128,32,128]{2,1,0:T(8,128)S(1)}, f32[128,32,128]{2,1,0:T(8,128)}, u32[]{:S(2)}) copy-start(f32[128,32,128]{2,1,0:T(8,128)} %param.6) | copy-start | bytes 6291460
  258.3 2.0 copy-start.1
Sparse Core Ops, SparseCore 0:
  66.5 123.2 all-reduce.3
  265.4 121.4 all-reduce.5
where the time goes:
time: 402 us; the launch traced here: 395 us
  waiting for transfers between devices  251 us (62%)
  other arithmetic  69.7 us (17%)
  matrix products  26.9 us (7%)
  local copies, waits for them, and re-layouts  22 us (5%)
  between operations  15.9 us (4%)
  starting transfers between devices  9.9 us (2%)
    psum x1, waiting for transfers between devices, body(): lax.psum(jnp.dot(stacked, stacked.T, precision=lax.Precision.HIGHEST), ('...  123 us
    psum x1, waiting for transfers between devices, body(): lax.psum(jnp.dot(new_basis, flat_carried.T, precision=lax.Precision.HIGHE...  117 us
    another operation x6, other arithmetic, body(): cholesky_low = jnp.linalg.cholesky(gram_matrix)  34 us
    another operation x3, other arithmetic, body(): jax.scipy.linalg.solve_triangular(cholesky_low, identity, lower=True)  19.7 us
    unnamed x24, local copies, waits for them, and re-layouts  17.4 us
  transfers between devices with their start and end apart: 10, of which 8 were waited for; matrix products, arithmetic and copies ran while one was open for 3% of the time, Pallas kernels for 0%

commit v1 on v0

--- a/solution.py
+++ b/solution.py
@@ -58,7 +58,10 @@
     inverse = jax.scipy.linalg.solve_triangular(cholesky_low, identity, lower=True)
     new_basis = jnp.dot(inverse, stacked, precision=lax.Precision.HIGHEST)
     galerkin = (
-        lax.psum(jnp.dot(new_basis, flat_carried.T, precision=lax.Precision.HIGHEST), ("gx", "gy"))
+        lax.psum(
+            lax.psum(jnp.dot(new_basis, flat_carried.T, precision=lax.Precision.HIGHEST), "gy"),
+            "gx",
+        )
         * cell_weight
     )
     return (new_basis.reshape(aug_count, tile_rows, tile_cols), galerkin)

time: 402 us -> 377 us (0.938)
  waiting for transfers between devices: 251 us -> 227 us
    psum x1, waiting for transfers between devices: 117 us -> 53.4 us  [body(): lax.psum(jnp.dot(new_basis, flat_carried.T, precision=lax.Precision.HIGHE...]
    psum x0 -> x1, waiting for transfers between devices: none -> 39.2 us  [body(): lax.psum(lax.psum(jnp.dot(new_basis, flat_carried.T, precision=lax.Precis...]
  transfers between devices with their start and end apart: 10 -> 11, of which waited for: 8 -> 9; matrix products, arithmetic and copies ran while one was open for 3% -> 3% of each run, Pallas kernels for 0% -> 0%
where the time goes in v1:
time: 377 us; the launch traced here: 371 us
  waiting for transfers between devices  227 us (60%)
  other arithmetic  69.7 us (18%)
  matrix products  26.9 us (7%)
  local copies, waits for them, and re-layouts  22 us (6%)
  between operations  15.6 us (4%)
  starting transfers between devices  9.94 us (3%)
    psum x1, waiting for transfers between devices, body(): lax.psum(jnp.dot(stacked, stacked.T, precision=lax.Precision.HIGHEST), ('...  123 us
    psum x1, waiting for transfers between devices, body(): lax.psum(jnp.dot(new_basis, flat_carried.T, precision=lax.Precision.HIGHE...  53.4 us
    psum x1, waiting for transfers between devices, body(): lax.psum(lax.psum(jnp.dot(new_basis, flat_carried.T, precision=lax.Precis...  39.2 us
    another operation x6, other arithmetic, body(): cholesky_low = jnp.linalg.cholesky(gram_matrix)  34 us
    another operation x3, other arithmetic, body(): jax.scipy.linalg.solve_triangular(cholesky_low, identity, lower=True)  19.7 us
    unnamed x24, local copies, waits for them, and re-layouts  17.4 us
  transfers between devices with their start and end apart: 11, of which 9 were waited for; matrix products, arithmetic and copies ran while one was open for 3% of the time, Pallas kernels for 0%

profile of v1, /device:TPU:0, one launch (start us, length us, event | category | flops | bytes accessed | tf_op | source)
XLA Modules:
  0.0 371.2 jit_solution(12774367034640296641)
XLA Ops:
  7.2 2.0 copy.49
  9.3 3.0 collective-permute-start.1
  13.3 3.5 copy.42
  17.0 1.9 pad_maximum_fusion.3
  18.9 2.7 collective-permute-start.2
  23.2 3.5 collective-permute-done.3
  26.7 2.7 add_multiply_fusion.1
  29.4 1.9 fusion.22
  31.3 1.9 convolution_subtract_fusion.1
  33.5 1.6 collective-permute-start.4
  35.6 2.2 collective-permute-done.4
  37.8 2.5 collective-permute-done.5
  41.2 3.0 copy.36
  44.2 1.6 collective-permute-done.7
  45.8 2.8 multiply_subtract_fusion
  48.6 1.8 fusion.23
  50.5 4.2 %add_multiply_fusion = f32[128,32,128]{0,2,1:T(8,128)S(1)} fusion(f32[128,1,128]{0,2,1:T(8,128)S(1)} %collective-permute-done.4, f32[128,32,128]{0,2,1:T(8,128)S(1)} %add.65, f32[128,1,128]{0,2,1:T(8,128)S(1)} %collective-permute-done.5, f32[128,34,1]{0,2,1:T(1,128)S(1)} %copy.51, f32[128,34,1]{0,2,1:T(1,128)S(1)} %copy.53, ...), kind=kLoop, calls=%fused_computation.23 | loop fusion | flops 7340032 | bytes 4392960 | tf_op jit(solution)/shard_map/add | solution.py:28
  54.7 1.9 convolution_subtract_fusion
  58.9 7.4 %fusion.1 = f32[256,256]{0,1:T(8,128)} fusion(f32[128,4096]{0,1:T(8,128)S(1)} %bitcast.71, f32[128,4096]{0,1:T(8,128)S(1)} %bitcast.75), kind=kOutput, calls=%fused_computation.6 | convolution fusion | flops 3222274048 | bytes 4456448 | tf_op jit(solution)/shard_map/dot_general | solution.py:54
  66.6 123.1 %all-reduce.5.cloned.1.call-done = f32[256,256]{0,1:T(8,128)} async-done(((f32[256,256]{0,1:T(8,128)}), f32[256,256]{0,1:T(8,128)}) %all-reduce.5.cloned.1.call-update) | async-done | bytes 262160 | tf_op jit(solution)/shard_map/psum | solution.py:54
  192.0 11.7 %cholesky.50 = f32[128,128]{1,0:T(8,128)S(1)} custom-call(f32[128,128]{1,0:T(8,128)S(1)} %cholesky.118), custom_call_target="Cholesky" | custom-call | tf_op jit(solution)/shard_map/jit(cholesky)/cholesky | solution.py:56
  203.8 9.8 %custom-call.15 = f32[1,128,128]{1,2,0:T(8,128)S(1)} custom-call(f32[1,128,128]{2,1,0:T(8,128)S(1)} %get-tuple-element.33), custom_call_target="InvertDiagBlocksLowerTriangular" | custom-call | tf_op jit(solution)/shard_map/jit(cholesky)/cholesky | solution.py:56
  214.1 11.7 %cholesky.105 = f32[128,128]{1,0:T(8,128)S(1)} custom-call(f32[128,128]{1,0:T(8,128)S(1)} %convolution_subtract_fusion.3), custom_call_target="Cholesky" | custom-call | tf_op jit(solution)/shard_map/jit(cholesky)/cholesky | solution.py:56
  227.9 4.1 %while.1 = (s32[]{:T(128)}, f32[256,256]{1,0:T(8,128)S(1)}, s32[2,2]{1,0:T(2,128)S(1)}, f32[2,128,128]{2,1,0:T(8,128)S(1)}, s32[]{:T(128)}) while((s32[]{:T(128)}, f32[256,256]{1,0:T(8,128)S(1)}, s32[2,2]{1,0:T(2,128)S(1)}, f32[2,128,128]{2,1,0:T(8,128)S(1)}, s32[]{:T(128)}) %tuple.33), condition=%wide.while_cond, body=%wide.while_body.sunk | while | flops 2 | bytes 131181 | solution.py:58
  232.0 19.7 %custom-call.16 = f32[2,128,128]{1,2,0:T(8,128)S(1)} custom-call(f32[2,128,128]{2,1,0:T(8,128)S(1)} %get-tuple-element.9), custom_call_target="InvertDiagBlocksLowerTriangular" | custom-call | tf_op jit(solution)/shard_map/jit(_solve_triangular)/triangular_solve | solution.py:58
  252.6 5.8 %fusion = f32[256,4096]{1,0:T(8,128)S(1)} fusion(f32[128,4096]{0,1:T(8,128)S(1)} %bitcast.72, f32[128,4096]{0,1:T(8,128)} %bitcast.74, f32[128,256]{1,0:T(8,128)S(1)} %fusion.12, f32[128,256]{1,0:T(8,128)S(1)} %fusion.9), kind=kOutput, calls=%fused_computation.5 | convolution fusion | flops 3222339584 | bytes 8650752 | tf_op jit(solution)/shard_map/dot_general | solution.py:59
  258.4 1.9 copy-done.1
  260.3 4.9 %fusion.2 = f32[256,128]{1,0:T(8,128)} fusion(f32[256,4096]{1,0:T(8,128)S(1)} %fusion, f32[16,8,32,128]{3,2,1,0:T(8,128)S(1)} %bitcast.65), kind=kOutput, calls=%fused_computation.8 | convolution fusion | flops 1610612736 | bytes 6422528 | tf_op jit(solution)/shard_map/dot_general | solution.py:62
  265.3 53.4 %all-reduce.7.cloned.1.call-done = f32[256,128]{1,0:T(8,128)} async-done(((f32[256,128]{1,0:T(8,128)}), f32[256,128]{1,0:T(8,128)}) %all-reduce.7.cloned.1.call-update) | async-done | bytes 131088 | tf_op jit(solution)/shard_map/psum | solution.py:62
  318.7 5.0 %copy.57 = f32[32,8,32,128]{3,2,1,0:T(8,128)} copy(f32[32,8,32,128]{3,1,2,0:T(8,128)} %bitcast.64) | data formatting | bytes 8388608
  323.7 39.2 %all-reduce.9.cloned.1.call-done = f32[256,128]{1,0:T(8,128)} async-done(((f32[256,128]{1,0:T(8,128)}), f32[256,128]{1,0:T(8,128)}) %all-reduce.9.cloned.1.call-update) | async-done | bytes 131088 | tf_op jit(solution)/shard_map/psum | solution.py:61
  362.8 1.6 broadcast_multiply_fusion.1
  (72 shorter events, 15.4 us)
Async XLA Ops:
  7.2 22.2 %copy-start = (f32[128,128]{1,0:T(8,128)S(1)}, f32[128,128]{1,0:T(8,128)}, u32[]{:S(2)}) copy-start(f32[128,128]{1,0:T(8,128)} %param.8) | copy-start | bytes 196612
  7.2 182.6 %all-reduce.5.cloned.1.call-start = ((), (), s32[]{:S(2)}) async-start(), calls=%async_computation | async-start | bytes 524288 | tf_op jit(solution)/shard_map/psum | solution.py:54
  9.2 17.4 %copy-start.2 = (f32[128,32,128]{0,2,1:T(8,128)}, f32[128,32,128]{0,2,1:T(8,128)S(1)}, u32[]{:S(2)}) copy-start(f32[128,32,128]{0,2,1:T(8,128)S(1)} %copy.49) | copy-start | bytes 6291460
  9.3 7.5 %collective-permute-start.1 = (f32[128,1,128]{0,2,1:T(8,128)S(1)}, f32[128,1,128]{0,2,1:T(8,128)S(1)}, u32[]{:S(2)}, u32[]{:S(2)}) collective-permute-start(f32[128,1,128]{0,2,1:T(8,128)S(1)} %get-tuple-element.28), channel_id=1, source_target_pairs={{0,8},{8,16},{16,24},{24,0},{1,9},{9,17},{17,25},{25,1},{2,10},{10... | collective-permute-start | bytes 196616 | tf_op jit(solution)/shard_map/ppermute | solution.py:14
  12.3 4.7 %collective-permute-start = (f32[128,1,128]{0,2,1:T(8,128)S(1)}, f32[128,1,128]{0,2,1:T(8,128)S(1)}, u32[]{:S(2)}, u32[]{:S(2)}) collective-permute-start(f32[128,1,128]{0,2,1:T(8,128)S(1)} %get-tuple-element.29), channel_id=1, source_target_pairs={{8,0},{16,8},{24,16},{0,24},{9,1},{17,9},{25,17},{1,25},{10,2},{18... | collective-permute-start | bytes 196616 | tf_op jit(solution)/shard_map/ppermute | solution.py:15
  17.0 4.7 %copy-start.9 = (f32[2,32,128]{2,1,0:T(8,128)S(1)}, f32[2,32,128]{2,1,0:T(8,128)}, u32[]{:S(2)}) copy-start(f32[2,32,128]{2,1,0:T(8,128)} %param.7) | copy-start | bytes 98308
  18.9 4.2 %collective-permute-start.2 = (f32[128,34,1]{0,1,2:T(8,128)S(1)}, f32[128,34,1]{0,1,2:T(8,128)S(1)}, u32[]{:S(2)}, u32[]{:S(2)}) collective-permute-start(f32[128,34,1]{0,1,2:T(8,128)S(1)} %get-tuple-element.23), channel_id=1, source_target_pairs={{1,0},{2,1},{3,2},{4,3},{5,4},{6,5},{7,6},{0,7},{9,8},{10,9},{11,1... | collective-permute-start | bytes 52232 | tf_op jit(solution)/shard_map/ppermute | solution.py:15
  21.7 5.0 %collective-permute-start.3 = (f32[128,34,1]{0,1,2:T(8,128)S(1)}, f32[128,34,1]{0,1,2:T(8,128)S(1)}, u32[]{:S(2)}, u32[]{:S(2)}) collective-permute-start(f32[128,34,1]{0,1,2:T(8,128)S(1)} %get-tuple-element.22), channel_id=1, source_target_pairs={{0,1},{1,2},{2,3},{3,4},{4,5},{5,6},{6,7},{7,0},{8,9},{9,10},{10,1... | collective-permute-start | bytes 52232 | tf_op jit(solution)/shard_map/ppermute | solution.py:14
  29.4 1.9 copy-start.8
  31.3 1.9 copy-start.3
  33.5 4.3 %collective-permute-start.4 = (f32[128,1,128]{0,2,1:T(8,128)S(1)}, f32[128,1,128]{0,2,1:T(8,128)S(1)}, u32[]{:S(2)}, u32[]{:S(2)}) collective-permute-start(f32[128,1,128]{0,2,1:T(8,128)S(1)} %get-tuple-element.27), channel_id=1, source_target_pairs={{8,0},{16,8},{24,16},{0,24},{9,1},{17,9},{25,17},{1,25},{10,2},{18... | collective-permute-start | bytes 196616 | tf_op jit(solution)/shard_map/ppermute | solution.py:15
  35.1 5.2 %collective-permute-start.5 = (f32[128,1,128]{0,2,1:T(8,128)S(1)}, f32[128,1,128]{0,2,1:T(8,128)S(1)}, u32[]{:S(2)}, u32[]{:S(2)}) collective-permute-start(f32[128,1,128]{0,2,1:T(8,128)S(1)} %get-tuple-element.26), channel_id=1, source_target_pairs={{0,8},{8,16},{16,24},{24,0},{1,9},{9,17},{17,25},{25,1},{2,10},{10... | collective-permute-start | bytes 196616 | tf_op jit(solution)/shard_map/ppermute | solution.py:14
  40.3 3.8 %collective-permute-start.6 = (f32[128,34,1]{0,1,2:T(8,128)S(1)}, f32[128,34,1]{0,1,2:T(8,128)S(1)}, u32[]{:S(2)}, u32[]{:S(2)}) collective-permute-start(f32[128,34,1]{0,1,2:T(8,128)S(1)} %copy.50), channel_id=1, source_target_pairs={{1,0},{2,1},{3,2},{4,3},{5,4},{6,5},{7,6},{0,7},{9,8},{10,9},{11,1... | collective-permute-start | bytes 52232 | tf_op jit(solution)/shard_map/ppermute | solution.py:15
  40.4 5.3 %collective-permute-start.7 = (f32[128,34,1]{0,1,2:T(8,128)S(1)}, f32[128,34,1]{0,1,2:T(8,128)S(1)}, u32[]{:S(2)}, u32[]{:S(2)}) collective-permute-start(f32[128,34,1]{0,1,2:T(8,128)S(1)} %copy.52), channel_id=1, source_target_pairs={{0,1},{1,2},{2,3},{3,4},{4,5},{5,6},{6,7},{7,0},{8,9},{9,10},{10,1... | collective-permute-start | bytes 52232 | tf_op jit(solution)/shard_map/ppermute | solution.py:14
  56.5 2.3 copy-start.7
  56.9 1.3 copy-start.5
  66.3 252.3 %all-reduce.7.cloned.1.call-start = ((), (), s32[]{:S(2)}) async-start(), calls=%async_computation.1 | async-start | bytes 262144 | tf_op jit(solution)/shard_map/psum | solution.py:62
  190.9 61.7 %copy-start.6 = (f32[128,32,128]{0,2,1:T(8,128)S(1)}, f32[128,32,128]{0,2,1:T(8,128)}, u32[]{:S(2)}) copy-start(f32[128,32,128]{0,2,1:T(8,128)} %copy-done.5) | copy-start | bytes 6291460
  252.6 7.8 %copy-start.4 = (f32[128,32,128]{2,1,0:T(8,128)S(1)}, f32[128,32,128]{2,1,0:T(8,128)}, u32[]{:S(2)}) copy-start(f32[128,32,128]{2,1,0:T(8,128)} %param.6) | copy-start | bytes 6291460
  258.3 2.0 copy-start.1
  265.3 97.6 %all-reduce.9.cloned.1.call-start = ((), (), s32[]{:S(2)}) async-start(), calls=%async_computation.2 | async-start | bytes 262144 | tf_op jit(solution)/shard_map/psum | solution.py:61
Sparse Core Ops, SparseCore 0:
  66.5 123.2 all-reduce.4
  265.4 53.2 all-reduce.6
  321.8 40.9 all-reduce.8
